TPU v7x, 256 devices: a whole 4x4x8 slice. The times are simulated.
256 devices in a mesh: row: 8 (over y, core), col: 32 (over z, x).
Axes of the slice: x: 4, y: 4, z: 8, core: 2. Of those that a mesh axis runs over, the one named last changes fastest.
Arguments:
- diag_block: float32 [1024, 1024], P('row')
- panel: bfloat16 [64, 1024, 1024], P('col', 'row'), may hold values from -1 to 1
- trailing: bfloat16 [32, 12, 1024, 1024], P('col', None, 'row'), may hold values from -6 to 6
- slot_rows: int32 [32, 12], replicated, may hold values from -1 to 63, as said below
- slot_cols: int32 [32, 12], replicated, may hold values from 0 to 1, as said below
Outputs:
- panel_factor: bfloat16 [64, 1024, 1024], P('col', 'row')
- updated: bfloat16 [32, 12, 1024, 1024], P('col', None, 'row')
Inputs may be any that keep to these rules, and one draw needn't show every extreme that they name: Slot s of grid column c holds the tile at tile row slot_rows[c, s] and tile column 2 * c + slot_cols[c, s] of the trailing matrix, or nothing where slot_rows[c, s] is -1. Live slots come first in each column; the pairs of one column are distinct and lie on or below the diagonal (tile row at least tile column). Within one grid column, live slots whose tile rows a and a' have a // 2 == a' // 2 have a == a'. Every column holds at least one live slot, column 0 fills all 12 slots and column 16 holds exactly one. `slot_cols`: 0 in empty slots.
All inputs are finite; a program needn't handle non-finite values.
Results may differ from a plain program's by a relative error of at most 0.0019.
Values may be sent and summed in bfloat16 or wider, within the bound.
No kernel may reach another device: no remote copies, remote signals or barrier semaphores. Data moves between devices by JAX's collectives and lax.ppermute only.
A program may use at most 128 MiB of HBM per device.

v0:
```python
import jax
import jax.numpy as jnp
from jax import lax
from jax.sharding import PartitionSpec as P


def slot_product(slices, left_ids, source_tiles, col_ids, position):
    left_slice = lax.dynamic_index_in_dim(slices, left_ids[position], 0, keepdims=False)
    right_tile = lax.dynamic_index_in_dim(source_tiles, col_ids[position], 0, keepdims=False)
    return lax.dot_general(
        left_slice, right_tile, (((1,), (1,)), ((), ())), preferred_element_type=jnp.float32
    )


def subtract_slot(buffer, position, update):
    previous = lax.dynamic_index_in_dim(buffer, position, 0, keepdims=False).astype(jnp.float32)
    return lax.dynamic_update_index_in_dim(
        buffer, (previous - update).astype(jnp.bfloat16), position, 0
    )


def local(diag_block, panel, trailing, slot_rows, slot_cols):
    diag_full = lax.all_gather(diag_block, "row", axis=0, tiled=True)
    factor = jnp.linalg.cholesky(diag_full)
    tile_count, row_count, tile_width = panel.shape
    stacked = panel.astype(jnp.float32).reshape(tile_count * row_count, tile_width)
    solved = lax.linalg.triangular_solve(factor, stacked.T, left_side=True, lower=True)
    panel_factor = solved.T.reshape(tile_count, row_count, tile_width).astype(jnp.bfloat16)
    whole_tiles = lax.all_gather(panel_factor, "row", axis=1, tiled=True)
    column_index = lax.axis_index("col")
    own_rows = lax.dynamic_index_in_dim(slot_rows, column_index, 0, keepdims=False)
    own_cols = lax.dynamic_index_in_dim(slot_cols, column_index, 0, keepdims=False)
    own_count = jnp.sum((own_rows >= 0).astype(jnp.int32))
    slices = lax.all_gather(panel_factor, "col", axis=0, tiled=True)

    def own_step(position, buffer):
        return subtract_slot(
            buffer, position, slot_product(slices, own_rows, whole_tiles, own_cols, position)
        )

    buffer = lax.fori_loop(0, own_count, own_step, trailing[0])
    return (panel_factor, buffer[None])


def solution(mesh):
    return jax.shard_map(
        local,
        mesh=mesh,
        in_specs=(P("row", None), P("col", "row", None), P("col", None, "row", None), P(), P()),
        out_specs=(P("col", "row", None), P("col", None, "row", None)),
        check_vma=False,
    )
```

profile of v0, /device:TPU:1, one launch (start us, length us, event | category | flops | bytes accessed | tf_op | source)
XLA Modules:
  0.0 681.8 jit_solution(6531067428901336610)
XLA Ops:
  9.6 43.7 %all-gather.4.cloned.1.call-done = f32[1024,1024]{0,1:T(8,128)} async-done(((f32[128,1024]{0,1:T(8,128)}), f32[1024,1024]{0,1:T(8,128)}) %all-gather.4.cloned.1.call-update) | async-done | bytes 4194320 | tf_op jit(solution)/shard_map/all_gather | solution.py:23
  53.3 5.3 copy.18
  58.7 4.4 fusion.18
  63.1 1.9 copy-done
  65.0 11.7 %cholesky.223 = f32[128,128]{1,0:T(8,128)S(1)} custom-call(f32[128,128]{1,0:T(8,128)S(1)} %cholesky.580), custom_call_target="Cholesky" | custom-call | tf_op jit(solution)/shard_map/jit(cholesky)/cholesky | solution.py:24
  76.8 9.8 %custom-call.62 = f32[1,128,128]{1,2,0:T(8,128)S(1)} custom-call(f32[1,128,128]{2,1,0:T(8,128)S(1)} %get-tuple-element.117), custom_call_target="InvertDiagBlocksLowerTriangular" | custom-call | tf_op jit(solution)/shard_map/jit(cholesky)/cholesky | solution.py:24
  86.6 2.5 cholesky.255
  89.1 2.4 constant_dynamic-update-slice_fusion.24
  91.5 1.5 convolution_subtract_fusion
  93.0 12.2 %cholesky.244 = f32[128,128]{1,0:T(8,128)S(1)} custom-call(f32[128,128]{1,0:T(8,128)S(1)} %cholesky.584), custom_call_target="Cholesky" | custom-call | tf_op jit(solution)/shard_map/jit(cholesky)/cholesky | solution.py:24
  105.8 9.8 %custom-call.63 = f32[1,128,128]{1,2,0:T(8,128)S(1)} custom-call(f32[1,128,128]{2,1,0:T(8,128)S(1)} %get-tuple-element.114), custom_call_target="InvertDiagBlocksLowerTriangular" | custom-call | tf_op jit(solution)/shard_map/jit(cholesky)/cholesky | solution.py:24
  116.9 2.1 convolution_subtract_fusion.1
  119.0 11.7 %cholesky.468 = f32[128,128]{1,0:T(8,128)S(1)} custom-call(f32[128,128]{1,0:T(8,128)S(1)} %cholesky.589), custom_call_target="Cholesky" | custom-call | tf_op jit(solution)/shard_map/jit(cholesky)/cholesky | solution.py:24
  132.0 9.8 %custom-call.64 = f32[1,128,128]{1,2,0:T(8,128)S(1)} custom-call(f32[1,128,128]{2,1,0:T(8,128)S(1)} %get-tuple-element.111), custom_call_target="InvertDiagBlocksLowerTriangular" | custom-call | tf_op jit(solution)/shard_map/jit(cholesky)/cholesky | solution.py:24
  143.0 2.3 convolution_subtract_fusion.2
  145.3 11.8 %cholesky.487 = f32[128,128]{1,0:T(8,128)S(1)} custom-call(f32[128,128]{1,0:T(8,128)S(1)} %cholesky.594), custom_call_target="Cholesky" | custom-call | tf_op jit(solution)/shard_map/jit(cholesky)/cholesky | solution.py:24
  158.5 9.8 %custom-call.65 = f32[1,128,128]{1,2,0:T(8,128)S(1)} custom-call(f32[1,128,128]{2,1,0:T(8,128)S(1)} %get-tuple-element.108), custom_call_target="InvertDiagBlocksLowerTriangular" | custom-call | tf_op jit(solution)/shard_map/jit(cholesky)/cholesky | solution.py:24
  169.4 2.3 convolution_subtract_fusion.3
  171.7 11.7 %cholesky.506 = f32[128,128]{1,0:T(8,128)S(1)} custom-call(f32[128,128]{1,0:T(8,128)S(1)} %cholesky.599), custom_call_target="Cholesky" | custom-call | tf_op jit(solution)/shard_map/jit(cholesky)/cholesky | solution.py:24
  184.7 10.0 %custom-call.66 = f32[1,128,128]{1,2,0:T(8,128)S(1)} custom-call(f32[1,128,128]{2,1,0:T(8,128)S(1)} %get-tuple-element.105), custom_call_target="InvertDiagBlocksLowerTriangular" | custom-call | tf_op jit(solution)/shard_map/jit(cholesky)/cholesky | solution.py:24
  195.8 2.3 convolution_subtract_fusion.4
  198.1 11.7 %cholesky.526 = f32[128,128]{1,0:T(8,128)S(1)} custom-call(f32[128,128]{1,0:T(8,128)S(1)} %cholesky.604), custom_call_target="Cholesky" | custom-call | tf_op jit(solution)/shard_map/jit(cholesky)/cholesky | solution.py:24
  211.0 9.8 %custom-call.67 = f32[1,128,128]{1,2,0:T(8,128)S(1)} custom-call(f32[1,128,128]{2,1,0:T(8,128)S(1)} %get-tuple-element.102), custom_call_target="InvertDiagBlocksLowerTriangular" | custom-call | tf_op jit(solution)/shard_map/jit(cholesky)/cholesky | solution.py:24
  221.7 2.0 convolution_subtract_fusion.11
  223.8 12.1 %cholesky.546 = f32[128,128]{1,0:T(8,128)S(1)} custom-call(f32[128,128]{1,0:T(8,128)S(1)} %cholesky.609), custom_call_target="Cholesky" | custom-call | tf_op jit(solution)/shard_map/jit(cholesky)/cholesky | solution.py:24
  237.2 9.8 %custom-call.68 = f32[1,128,128]{1,2,0:T(8,128)S(1)} custom-call(f32[1,128,128]{2,1,0:T(8,128)S(1)} %get-tuple-element.99), custom_call_target="InvertDiagBlocksLowerTriangular" | custom-call | tf_op jit(solution)/shard_map/jit(cholesky)/cholesky | solution.py:24
  247.9 1.8 convolution_subtract_fusion.13
  249.7 11.7 %cholesky.564 = f32[128,128]{1,0:T(8,128)S(1)} custom-call(f32[128,128]{1,0:T(8,128)S(1)} %convolution_subtract_fusion.13), custom_call_target="Cholesky" | custom-call | tf_op jit(solution)/shard_map/jit(cholesky)/cholesky | solution.py:24
  268.3 4.8 select_select_fusion
  273.1 23.0 %while.12 = (s32[]{:T(128)}, f32[1024,1024]{1,0:T(8,128)}, s32[8,2]{0,1:T(2,128)S(1)}, f32[8,128,128]{2,1,0:T(8,128)S(1)}, s32[]{:T(128)}) while((s32[]{:T(128)}, f32[1024,1024]{1,0:T(8,128)}, s32[8,2]{0,1:T(2,128)S(1)}, f32[8,128,128]{2,1,0:T(8,128)S(1)}, s32[]{:T(128)}) %tuple.74), condition=%wide.while_cond, body=%wide.while_body.sunk | while | flops 2 | bytes 131189 | solution.py:27
  273.7 2.3 bitcast_dynamic-update-slice_fusion.2
  276.6 2.3 bitcast_dynamic-update-slice_fusion.2
  279.5 2.3 bitcast_dynamic-update-slice_fusion.2
  282.4 2.3 bitcast_dynamic-update-slice_fusion.2
  285.2 2.3 bitcast_dynamic-update-slice_fusion.2
  288.1 2.3 bitcast_dynamic-update-slice_fusion.2
  291.0 2.3 bitcast_dynamic-update-slice_fusion.2
  293.9 2.2 bitcast_dynamic-update-slice_fusion.2
  296.1 78.8 %custom-call.69 = f32[8,128,128]{1,2,0:T(8,128)S(1)} custom-call(f32[8,128,128]{2,1,0:T(8,128)S(1)} %get-tuple-element.48), custom_call_target="InvertDiagBlocksLowerTriangular" | custom-call | tf_op jit(solution)/shard_map/triangular_solve | solution.py:27
  380.0 1.3 convolution_subtract_fusion.7
  382.2 1.4 convolution_subtract_fusion.6
  384.7 1.7 convolution_subtract_fusion.5
  386.4 1.8 convert_dynamic-update-slice_fusion.1
  388.2 1.5 convolution_subtract_fusion.9
  389.7 1.8 convert_dynamic-update-slice_fusion
  391.5 1.7 convolution_subtract_fusion.12
  393.2 1.8 fusion.19
  394.9 2.0 copy.24
  398.6 34.2 %all-gather.8.cloned.1.call-done = bf16[2,1024,1024]{2,1,0:T(8,128)(2,1)} async-done(((bf16[2,128,1024]{2,1,0:T(8,128)(2,1)}), bf16[2,1024,1024]{2,1,0:T(8,128)(2,1)}) %all-gather.8.cloned.1.call-update) | async-done | bytes 4194320 | tf_op jit(solution)/shard_map/all_gather | solution.py:29
  432.8 142.9 %all-gather.6.cloned.1.call-done = bf16[64,128,1024]{2,1,0:T(8,128)(2,1)} async-done(((bf16[2,128,1024]{2,1,0:T(8,128)(2,1)}), bf16[64,128,1024]{2,1,0:T(8,128)(2,1)}) %all-gather.6.cloned.1.call-update) | async-done | bytes 16777232 | tf_op jit(solution)/shard_map/all_gather | solution.py:34
  575.8 97.6 %while.11 = (s32[]{:T(128)}, bf16[12,128,1024]{2,1,0:T(8,128)(2,1)S(1)}, s32[]{:T(128)}, s32[12]{0:T(128)S(1)}, bf16[64,128,1024]{2,1,0:T(8,128)(2,1)}, /*index=...) while((s32[]{:T(128)}, ...), condition=%wide.region_18.19_spmd, body=%wide.region_17.18_spmd.sunk | while | flops 268828672 | bytes 3408139 | solution.py:41
  581.3 2.5 fusion.100
  589.4 2.5 fusion.100
  597.5 2.5 fusion.100
  605.6 2.5 fusion.100
  613.6 2.5 fusion.100
  621.7 2.5 fusion.100
  629.8 2.5 fusion.100
  637.9 2.5 fusion.100
  646.0 2.5 fusion.100
  654.1 2.5 fusion.100
  662.1 2.5 fusion.100
  670.2 2.5 fusion.100
  673.4 1.7 copy-done.1
  (124 shorter events, 45.9 us)
Async XLA Ops:
  7.2 1.0 copy-start.4
  7.2 2.1 copy-start.5
  7.2 46.1 %all-gather.4.cloned.1.call-start = ((), (), s32[]{:S(2)}) async-start(), calls=%async_computation | async-start | bytes 4718592 | tf_op jit(solution)/shard_map/all_gather | solution.py:23
  9.2 423.6 %all-gather.8.cloned.1.call-start = ((), (), s32[]{:S(2)}) async-start(), calls=%async_computation.2 | async-start | bytes 4718592 | tf_op jit(solution)/shard_map/all_gather | solution.py:29
  9.6 372.6 %copy-start.3 = (f32[1024,256]{1,0:T(8,128)}, f32[1024,256]{1,0:T(8,128)S(1)}, u32[]{:S(2)}) copy-start(f32[1024,256]{1,0:T(8,128)S(1)} %bitcast_convert_fusion) | copy-start | bytes 3145732
  63.1 1.9 copy-start
  374.9 9.7 %copy-start.6 = (f32[8,128,128]{1,2,0:T(8,128)}, f32[8,128,128]{1,2,0:T(8,128)S(1)}, u32[]{:S(2)}) copy-start(f32[8,128,128]{1,2,0:T(8,128)S(1)} %custom-call.69) | copy-start | bytes 1572868
  384.7 13.1 %copy-start.7 = (s32[32,12]{0,1:T(8,128)S(1)}, s32[32,12]{0,1:T(8,128)}, u32[]{:S(2)}) copy-start(s32[32,12]{0,1:T(8,128)} %param.11) | copy-start | bytes 4612
  384.7 13.1 %copy-start.8 = (s32[32,12]{0,1:T(8,128)S(1)}, s32[32,12]{0,1:T(8,128)}, u32[]{:S(2)}) copy-start(s32[32,12]{0,1:T(8,128)} %param.10) | copy-start | bytes 4612
  384.7 191.1 %copy-start.2 = (bf16[1,12,128,1024]{3,2,1,0:T(8,128)(2,1)S(1)}, bf16[1,12,128,1024]{3,2,1,0:T(8,128)(2,1)}, u32[]{:S(2)}) copy-start(bf16[1,12,128,1024]{3,2,1,0:T(8,128)(2,1)} %param.9) | copy-start | bytes 9437188
  397.0 178.7 %all-gather.6.cloned.1.call-start = ((), (), s32[]{:S(2)}) async-start(), calls=%async_computation.1 | async-start | bytes 17301504 | tf_op jit(solution)/shard_map/all_gather | solution.py:34
  673.4 1.7 copy-start.1
Sparse Core Ops, SparseCore 0:
  10.4 42.8 all-gather.3
  397.1 35.6 all-gather.7
  436.0 139.6 all-gather.5
where the time goes:
time: 693 us; the launch traced here: 682 us
  other arithmetic  261 us (38%)
  waiting for transfers between devices  222 us (32%)
  matrix products  73.2 us (11%)
  local copies, waits for them, and re-layouts  53.5 us (8%)
  loops' own time  52.9 us (8%)
  between operations  19.3 us (3%)
    another operation x30, other arithmetic, local(): factor = jnp.linalg.cholesky(diag_full)  173 us
    all_gather x1, waiting for transfers between devices, local(): slices = lax.all_gather(panel_factor, 'col', axis=0, tiled=True)  143 us
    another operation x3, other arithmetic, local(): lax.linalg.triangular_solve(factor, stacked.T, left_side=True, lower=True)  83.6 us
    another operation x1, loops' own time, local(): buffer = lax.fori_loop(0, own_count, own_step, trailing[0])  52.7 us
    all_gather x1, waiting for transfers between devices, local(): diag_full = lax.all_gather(diag_block, 'row', axis=0, tiled=True)  43.7 us
    all_gather x1, waiting for transfers between devices, local(): whole_tiles = lax.all_gather(panel_factor, 'row', axis=1, tiled=True)  34.2 us
    dot_general x12, matrix products, slot_product(): lax.dot_general(left_slice, right_tile, (((1,), (1,)), ((), ())), preferr...  30.3 us
    another operation x14, matrix products, local(): factor = jnp.linalg.cholesky(diag_full)  23.1 us
  transfers between devices with their start and end apart: 3, of which 3 were waited for; matrix products, arithmetic and copies ran while one was open for 0% of the time, Pallas kernels for 0%

commit v1 on v0

--- a/solution.py
+++ b/solution.py
@@ -20,7 +20,21 @@
 
 
 def local(diag_block, panel, trailing, slot_rows, slot_cols):
-    diag_full = lax.all_gather(diag_block, "row", axis=0, tiled=True)
+    ways, here, turn = (lax.axis_size("row"), lax.axis_index("row"), diag_block.shape[0])
+    shape = [n * ways if d == 0 else n for d, n in enumerate(diag_block.shape)]
+    full = lax.dynamic_update_slice_in_dim(
+        jnp.zeros(shape, diag_block.dtype), diag_block, here * turn, axis=0
+    )
+    going_up = going_down = diag_block
+    for far in range(1, ways // 2 + 1):
+        going_up = lax.ppermute(going_up, "row", [(d, (d + 1) % ways) for d in range(ways)])
+        full = lax.dynamic_update_slice_in_dim(full, going_up, (here - far) % ways * turn, axis=0)
+        if 2 * far < ways:
+            going_down = lax.ppermute(going_down, "row", [(d, (d - 1) % ways) for d in range(ways)])
+            full = lax.dynamic_update_slice_in_dim(
+                full, going_down, (here + far) % ways * turn, axis=0
+            )
+    diag_full = full
     factor = jnp.linalg.cholesky(diag_full)
     tile_count, row_count, tile_width = panel.shape
     stacked = panel.astype(jnp.float32).reshape(tile_count * row_count, tile_width)

time: 693 us -> 702 us (1.013)
  waiting for transfers between devices: 222 us -> 192 us
  local copies, waits for them, and re-layouts: 53.5 us -> 76.8 us
  starting transfers between devices: 0.12 us -> 13.2 us
    all_gather x1 -> x0, waiting for transfers between devices: 43.7 us -> none  [local(): diag_full = lax.all_gather(diag_block, 'row', axis=0, tiled=True)]
    dynamic_update_slice x0 -> x9, local copies, waits for them, and re-layouts: none -> 16.5 us  [the longest x5 12 us: local(): lax.dynamic_update_slice_in_dim(full, going_up, (here - far) % ways * tur...]
    ppermute x0 -> x7, starting transfers between devices: none -> 13.1 us  [the longest x4 7.98 us: local(): lax.ppermute(going_up, 'row', [(d, (d + 1) % ways) for d in range(ways)])]
    ppermute x0 -> x7, waiting for transfers between devices: none -> 10.2 us  [the longest x4 9.89 us: local(): lax.ppermute(going_up, 'row', [(d, (d + 1) % ways) for d in range(ways)])]
    another operation x24 -> x40, local copies, waits for them, and re-layouts: 22.8 us -> 28.5 us
  transfers between devices with their start and end apart: 3 -> 9, of which waited for: 3 -> 5; matrix products, arithmetic and copies ran while one was open for 0% -> 2% of each run, Pallas kernels for 0% -> 0%
where the time goes in v1:
time: 702 us; the launch traced here: 690 us
  other arithmetic  257 us (37%)
  waiting for transfers between devices  192 us (27%)
  matrix products  77.6 us (11%)
  local copies, waits for them, and re-layouts  76.8 us (11%)
  loops' own time  52.8 us (8%)
  between operations  19.7 us (3%)
  starting transfers between devices  13.2 us (2%)
    another operation x30, other arithmetic, local(): factor = jnp.linalg.cholesky(diag_full)  168 us
    all_gather x1, waiting for transfers between devices, local(): slices = lax.all_gather(panel_factor, 'col', axis=0, tiled=True)  143 us
    another operation x3, other arithmetic, local(): lax.linalg.triangular_solve(factor, stacked.T, left_side=True, lower=True)  84.4 us
    another operation x1, loops' own time, local(): buffer = lax.fori_loop(0, own_count, own_step, trailing[0])  52.7 us
    all_gather x1, waiting for transfers between devices, local(): whole_tiles = lax.all_gather(panel_factor, 'row', axis=1, tiled=True)  38.3 us
    dot_general x12, matrix products, slot_product(): lax.dot_general(left_slice, right_tile, (((1,), (1,)), ((), ())), preferr...  30.3 us
    another operation x40, local copies, waits for them, and re-layouts  28.5 us
    another operation x14, matrix products, local(): factor = jnp.linalg.cholesky(diag_full)  26.1 us
  transfers between devices with their start and end apart: 9, of which 5 were waited for; matrix products, arithmetic and copies ran while one was open for 2% of the time, Pallas kernels for 0%

profile of v1, /device:TPU:1, one launch (start us, length us, event | category | flops | bytes accessed | tf_op | source)
XLA Modules:
  0.0 689.7 jit_solution(12529706108527238729)
XLA Ops:
  8.4 2.7 collective-permute-start
  11.7 5.5 collective-permute-done
  17.2 2.5 collective-permute-start.2
  21.5 4.3 collective-permute-done.2
  25.8 2.6 collective-permute-start.4
  28.7 2.5 broadcast_in_dim.12
  32.1 3.0 collective-permute-start.5
  35.2 2.0 constant_dynamic-update-slice_fusion.25
  38.2 1.9 constant_dynamic-update-slice_fusion.23
  40.1 1.9 constant_dynamic-update-slice_fusion.22
  42.0 1.9 constant_dynamic-update-slice_fusion.21
  45.7 5.3 copy.56
  51.0 4.4 fusion.18
  55.5 1.9 copy-done.1
  57.4 11.7 %cholesky.222 = f32[128,128]{1,0:T(8,128)S(1)} custom-call(f32[128,128]{1,0:T(8,128)S(1)} %cholesky.577), custom_call_target="Cholesky" | custom-call | tf_op jit(solution)/shard_map/jit(cholesky)/cholesky | solution.py:38
  69.2 9.8 %custom-call.62 = f32[1,128,128]{1,2,0:T(8,128)S(1)} custom-call(f32[1,128,128]{2,1,0:T(8,128)S(1)} %get-tuple-element.121), custom_call_target="InvertDiagBlocksLowerTriangular" | custom-call | tf_op jit(solution)/shard_map/jit(cholesky)/cholesky | solution.py:38
  82.4 11.7 %cholesky.243 = f32[128,128]{1,0:T(8,128)S(1)} custom-call(f32[128,128]{1,0:T(8,128)S(1)} %cholesky.581), custom_call_target="Cholesky" | custom-call | tf_op jit(solution)/shard_map/jit(cholesky)/cholesky | solution.py:38
  94.7 9.8 %custom-call.63 = f32[1,128,128]{1,2,0:T(8,128)S(1)} custom-call(f32[1,128,128]{2,1,0:T(8,128)S(1)} %get-tuple-element.119), custom_call_target="InvertDiagBlocksLowerTriangular" | custom-call | tf_op jit(solution)/shard_map/jit(cholesky)/cholesky | solution.py:38
  105.6 2.0 copy-done
  107.6 2.4 slice_subtract_fusion.1
  110.0 11.7 %cholesky.466 = f32[128,128]{1,0:T(8,128)S(1)} custom-call(f32[128,128]{1,0:T(8,128)S(1)} %cholesky.586), custom_call_target="Cholesky" | custom-call | tf_op jit(solution)/shard_map/jit(cholesky)/cholesky | solution.py:38
  122.5 9.8 %custom-call.64 = f32[1,128,128]{1,2,0:T(8,128)S(1)} custom-call(f32[1,128,128]{2,1,0:T(8,128)S(1)} %get-tuple-element.117), custom_call_target="InvertDiagBlocksLowerTriangular" | custom-call | tf_op jit(solution)/shard_map/jit(cholesky)/cholesky | solution.py:38
  133.6 3.3 slice_subtract_fusion.2
  136.9 11.7 %cholesky.485 = f32[128,128]{1,0:T(8,128)S(1)} custom-call(f32[128,128]{1,0:T(8,128)S(1)} %cholesky.591), custom_call_target="Cholesky" | custom-call | tf_op jit(solution)/shard_map/jit(cholesky)/cholesky | solution.py:38
  149.4 9.8 %custom-call.65 = f32[1,128,128]{1,2,0:T(8,128)S(1)} custom-call(f32[1,128,128]{2,1,0:T(8,128)S(1)} %get-tuple-element.115), custom_call_target="InvertDiagBlocksLowerTriangular" | custom-call | tf_op jit(solution)/shard_map/jit(cholesky)/cholesky | solution.py:38
  160.3 3.2 slice_subtract_fusion.3
  163.5 11.9 %cholesky.504 = f32[128,128]{1,0:T(8,128)S(1)} custom-call(f32[128,128]{1,0:T(8,128)S(1)} %cholesky.596), custom_call_target="Cholesky" | custom-call | tf_op jit(solution)/shard_map/jit(cholesky)/cholesky | solution.py:38
  176.1 9.8 %custom-call.66 = f32[1,128,128]{1,2,0:T(8,128)S(1)} custom-call(f32[1,128,128]{2,1,0:T(8,128)S(1)} %get-tuple-element.113), custom_call_target="InvertDiagBlocksLowerTriangular" | custom-call | tf_op jit(solution)/shard_map/jit(cholesky)/cholesky | solution.py:38
  187.1 3.1 slice_subtract_fusion.4
  190.2 11.7 %cholesky.524 = f32[128,128]{1,0:T(8,128)S(1)} custom-call(f32[128,128]{1,0:T(8,128)S(1)} %cholesky.601), custom_call_target="Cholesky" | custom-call | tf_op jit(solution)/shard_map/jit(cholesky)/cholesky | solution.py:38
  202.7 9.8 %custom-call.67 = f32[1,128,128]{1,2,0:T(8,128)S(1)} custom-call(f32[1,128,128]{2,1,0:T(8,128)S(1)} %get-tuple-element.111), custom_call_target="InvertDiagBlocksLowerTriangular" | custom-call | tf_op jit(solution)/shard_map/jit(cholesky)/cholesky | solution.py:38
  213.5 3.1 slice_subtract_fusion.5
  216.5 11.7 %cholesky.544 = f32[128,128]{1,0:T(8,128)S(1)} custom-call(f32[128,128]{1,0:T(8,128)S(1)} %cholesky.606), custom_call_target="Cholesky" | custom-call | tf_op jit(solution)/shard_map/jit(cholesky)/cholesky | solution.py:38
  229.0 9.8 %custom-call.68 = f32[1,128,128]{1,2,0:T(8,128)S(1)} custom-call(f32[1,128,128]{2,1,0:T(8,128)S(1)} %get-tuple-element.109), custom_call_target="InvertDiagBlocksLowerTriangular" | custom-call | tf_op jit(solution)/shard_map/jit(cholesky)/cholesky | solution.py:38
  239.8 2.1 slice_subtract_fusion.6
  241.9 11.7 %cholesky.562 = f32[128,128]{1,0:T(8,128)S(1)} custom-call(f32[128,128]{1,0:T(8,128)S(1)} %slice_subtract_fusion.6), custom_call_target="Cholesky" | custom-call | tf_op jit(solution)/shard_map/jit(cholesky)/cholesky | solution.py:38
  263.9 4.8 select_select_fusion
  268.8 28.6 %while.12 = (s32[]{:T(128)}, f32[1024,1024]{0,1:T(8,128)}, s32[8,2]{0,1:T(2,128)S(1)}, f32[8,128,128]{2,1,0:T(8,128)}, s32[]{:T(128)}) while((s32[]{:T(128)}, f32[1024,1024]{0,1:T(8,128)}, s32[8,2]{0,1:T(2,128)S(1)}, f32[8,128,128]{2,1,0:T(8,128)}, s32[]{:T(128)}) %tuple.69), condition=%wide.while_cond, body=%wide.while_body.sunk | while | flops 2 | bytes 393329 | solution.py:41
  269.4 2.3 dynamic-slice.7
  273.0 2.3 dynamic-slice.7
  276.6 2.3 dynamic-slice.7
  280.1 2.3 dynamic-slice.7
  283.7 2.3 dynamic-slice.7
  287.3 2.3 dynamic-slice.7
  290.9 2.3 dynamic-slice.7
  294.5 2.2 dynamic-slice.7
  297.4 79.5 %custom-call.69 = f32[8,128,128]{1,2,0:T(8,128)S(1)} custom-call(f32[8,128,128]{2,1,0:T(8,128)} %get-tuple-element.48), custom_call_target="InvertDiagBlocksLowerTriangular" | custom-call | tf_op jit(solution)/shard_map/triangular_solve | solution.py:41
  394.6 2.0 convolution_subtract_fusion.6
  398.4 2.0 copy.84
  402.1 38.3 %all-gather.5.cloned.1.call-done = bf16[2,1024,1024]{2,1,0:T(8,128)(2,1)} async-done(((bf16[2,128,1024]{2,1,0:T(8,128)(2,1)}), bf16[2,1024,1024]{2,1,0:T(8,128)(2,1)}) %all-gather.5.cloned.1.call-update) | async-done | bytes 4194320 | tf_op jit(solution)/shard_map/all_gather | solution.py:43
  440.5 142.9 %all-gather.3.cloned.1.call-done = bf16[64,128,1024]{2,1,0:T(8,128)(2,1)} async-done(((bf16[2,128,1024]{2,1,0:T(8,128)(2,1)}), bf16[64,128,1024]{2,1,0:T(8,128)(2,1)}) %all-gather.3.cloned.1.call-update) | async-done | bytes 16777232 | tf_op jit(solution)/shard_map/all_gather | solution.py:48
  583.4 97.6 %while.11 = (s32[]{:T(128)}, bf16[12,128,1024]{2,1,0:T(8,128)(2,1)S(1)}, s32[]{:T(128)}, s32[12]{0:T(128)S(1)}, bf16[64,128,1024]{2,1,0:T(8,128)(2,1)}, /*index=...) while((s32[]{:T(128)}, ...), condition=%wide.region_18.19_spmd, body=%wide.region_17.18_spmd.sunk | while | flops 268828672 | bytes 3408139 | solution.py:55
  588.9 2.5 fusion.117
  597.0 2.5 fusion.117
  605.1 2.5 fusion.117
  613.2 2.5 fusion.117
  621.3 2.5 fusion.117
  629.3 2.5 fusion.117
  637.4 2.5 fusion.117
  645.5 2.5 fusion.117
  653.6 2.5 fusion.117
  661.7 2.5 fusion.117
  669.8 2.5 fusion.117
  677.9 2.5 fusion.117
  (181 shorter events, 75.1 us)
Async XLA Ops:
  7.2 1.0 copy-start.5
  7.2 21.3 %copy-start.6 = (bf16[2,128,1024]{2,1,0:T(8,128)(2,1)S(1)}, bf16[2,128,1024]{2,1,0:T(8,128)(2,1)}, u32[]{:S(2)}) copy-start(bf16[2,128,1024]{2,1,0:T(8,128)(2,1)} %param.8) | copy-start | bytes 1572868
  7.2 433.3 %all-gather.5.cloned.1.call-start = ((), (), s32[]{:S(2)}) async-start(), calls=%async_computation.1 | async-start | bytes 4718592 | tf_op jit(solution)/shard_map/all_gather | solution.py:43
  8.4 8.8 %collective-permute-start = (f32[128,1024]{0,1:T(8,128)S(1)}, f32[128,1024]{0,1:T(8,128)S(1)}, u32[]{:S(2)}, u32[]{:S(2)}) collective-permute-start(f32[128,1024]{0,1:T(8,128)S(1)} %copy.53), channel_id=1, source_target_pairs={{0,32},{32,64},{64,96},{96,128},{128,160},{160,192},{192,224},{224... | collective-permute-start | bytes 1572872 | tf_op jit(solution)/shard_map/ppermute | solution.py:30
  11.1 8.9 %collective-permute-start.1 = (f32[128,1024]{0,1:T(8,128)S(1)}, f32[128,1024]{0,1:T(8,128)S(1)}, u32[]{:S(2)}, u32[]{:S(2)}) collective-permute-start(f32[128,1024]{0,1:T(8,128)S(1)} %copy.53), channel_id=1, source_target_pairs={{0,224},{32,0},{64,32},{96,64},{128,96},{160,128},{192,160},{224,1... | collective-permute-start | bytes 1572872 | tf_op jit(solution)/shard_map/ppermute | solution.py:33
  17.2 13.9 %copy-start.7 = (f32[128,1024]{0,1:T(8,128)}, f32[128,1024]{0,1:T(8,128)S(1)}, u32[]{:S(2)}) copy-start(f32[128,1024]{0,1:T(8,128)S(1)} %collective-permute-done) | copy-start | bytes 1572868
  17.2 8.6 %collective-permute-start.2 = (f32[128,1024]{0,1:T(8,128)S(1)}, f32[128,1024]{0,1:T(8,128)}, u32[]{:S(2)}, u32[]{:S(2)}) collective-permute-start(f32[128,1024]{0,1:T(8,128)S(1)} %collective-permute-done), channel_id=1, source_target_pairs={{0,32},{32,64},{64,96},{96,128},{128,160},{160,192},{192,224},{224... | collective-permute-start | bytes 1572872 | tf_op jit(solution)/shard_map/ppermute | solution.py:30
  20.0 12.1 %collective-permute-start.3 = (f32[128,1024]{0,1:T(8,128)S(1)}, f32[128,1024]{0,1:T(8,128)}, u32[]{:S(2)}, u32[]{:S(2)}) collective-permute-start(f32[128,1024]{0,1:T(8,128)S(1)} %collective-permute-done.1), channel_id=1, source_target_pairs={{0,224},{32,0},{64,32},{96,64},{128,96},{160,128},{192,160},{224,1... | collective-permute-start | bytes 1572872 | tf_op jit(solution)/shard_map/ppermute | solution.py:33
  25.8 11.3 %collective-permute-start.4 = (f32[128,1024]{0,1:T(8,128)}, f32[128,1024]{0,1:T(8,128)}, u32[]{:S(2)}, u32[]{:S(2)}) collective-permute-start(f32[128,1024]{0,1:T(8,128)} %collective-permute-done.2), channel_id=1, source_target_pairs={{0,32},{32,64},{64,96},{96,128},{128,160},{160,192},{192,224},{224... | collective-permute-start | bytes 1572872 | tf_op jit(solution)/shard_map/ppermute | solution.py:30
  32.1 352.5 %copy-start.4 = (f32[1024,256]{1,0:T(8,128)}, f32[1024,256]{1,0:T(8,128)S(1)}, u32[]{:S(2)}) copy-start(f32[1024,256]{1,0:T(8,128)S(1)} %bitcast_convert_fusion) | copy-start | bytes 3145732
  32.1 11.8 %collective-permute-start.5 = (f32[128,1024]{0,1:T(8,128)}, f32[128,1024]{0,1:T(8,128)S(1)}, u32[]{:S(2)}, u32[]{:S(2)}) collective-permute-start(f32[128,1024]{0,1:T(8,128)} %collective-permute-done.3), channel_id=1, source_target_pairs={{0,224},{32,0},{64,32},{96,64},{128,96},{160,128},{192,160},{224,1... | collective-permute-start | bytes 1572872 | tf_op jit(solution)/shard_map/ppermute | solution.py:33
  37.1 7.7 %collective-permute-start.6 = (f32[128,1024]{0,1:T(8,128)}, f32[128,1024]{0,1:T(8,128)S(1)}, u32[]{:S(2)}, u32[]{:S(2)}) collective-permute-start(f32[128,1024]{0,1:T(8,128)} %collective-permute-done.4), channel_id=1, source_target_pairs={{0,32},{32,64},{64,96},{96,128},{128,160},{160,192},{192,224},{224... | collective-permute-start | bytes 1572872 | tf_op jit(solution)/shard_map/ppermute | solution.py:30
  55.4 1.9 copy-start.1
  105.6 2.0 copy-start
  377.0 10.2 %copy-start.8 = (f32[8,128,128]{1,2,0:T(8,128)}, f32[8,128,128]{1,2,0:T(8,128)S(1)}, u32[]{:S(2)}) copy-start(f32[8,128,128]{1,2,0:T(8,128)S(1)} %custom-call.69) | copy-start | bytes 1572868
  387.2 14.0 %copy-start.9 = (s32[32,12]{0,1:T(8,128)S(1)}, s32[32,12]{0,1:T(8,128)}, u32[]{:S(2)}) copy-start(s32[32,12]{0,1:T(8,128)} %param.11) | copy-start | bytes 4612
  387.3 14.0 %copy-start.10 = (s32[32,12]{0,1:T(8,128)S(1)}, s32[32,12]{0,1:T(8,128)}, u32[]{:S(2)}) copy-start(s32[32,12]{0,1:T(8,128)} %param.10) | copy-start | bytes 4612
  387.3 196.1 %copy-start.3 = (bf16[1,12,128,1024]{3,2,1,0:T(8,128)(2,1)S(1)}, bf16[1,12,128,1024]{3,2,1,0:T(8,128)(2,1)}, u32[]{:S(2)}) copy-start(bf16[1,12,128,1024]{3,2,1,0:T(8,128)(2,1)} %param.9) | copy-start | bytes 9437188
  400.5 182.9 %all-gather.3.cloned.1.call-start = ((), (), s32[]{:S(2)}) async-start(), calls=%async_computation | async-start | bytes 17301504 | tf_op jit(solution)/shard_map/all_gather | solution.py:48
  681.0 1.7 copy-start.2
Sparse Core Ops, SparseCore 0:
  400.6 39.8 all-gather.4
  443.6 139.6 all-gather.2
